TPU v7x, 32 devices: a whole 2x2x4 slice. The times are simulated.
32 devices in a mesh: groups: 2 (over y), gx: 8 (over z, x), gy: 2 (over core).
Axes of the slice: x: 2, y: 2, z: 4, core: 2. Of those that a mesh axis runs over, the one named last changes fastest.
Arguments:
- probe_vectors: bfloat16 [8192, 1536], P(('groups', 'gx', 'gy')), parts along dimension 0, may hold values from -60 to 60
- mesh_lookup_pair: bfloat16 [8192, 2, 1536], P(('groups', 'gx', 'gy')), parts along dimension 0, may hold values from -6 to 6
- landmark_lookup_pair: bfloat16 [128, 2, 1536], P(('groups', 'gx', 'gy')), parts along dimension 0, may hold values from -6 to 6
- softmax_warmth: float32 [24], P('groups'), parts along dimension 0, may hold values from 0.5 to 2
- output_adjoint: bfloat16 [8192, 1536], P(('groups', 'gx', 'gy')), parts along dimension 0, may hold values from -6 to 6
- exported_boundary_tiles: int32 [32, 3, 1], P(('groups', 'gx', 'gy')), parts along dimension 0, may hold values from 0 to 1
- adjacency_tile_filter: int32 [32, 2, 5], P(('groups', 'gx', 'gy')), parts along dimension 0, may hold values 0 or 1
Outputs:
- probe_derivative: bfloat16 [8192, 1536], P(('groups', 'gx', 'gy')), parts along dimension 0
- cell_kv_grad: bfloat16 [8192, 2, 1536], P(('groups', 'gx', 'gy')), parts along dimension 0
- anchor_kv_grad: float32 [128, 2, 1536], P(('groups', 'gx', 'gy')), parts along dimension 0
- temperature_grad: float32 [24], P('groups'), parts along dimension 0
There are 2 independent parts, one for each index of `groups`. A program takes and returns all parts, laid end to end along the dimension named above; each array names one. Nothing has to cross between parts.
All inputs are finite; a program needn't handle non-finite values. No bound on the sum of `adjacency_tile_filter` on one device may be relied on, other than what follows from the above.
Results may differ from a plain program's by a relative error of at most 0.001.
The roundings to bfloat16 on the way count: a program that leaves them out, or rounds other values in their place, can miss the bound.
Values may be sent and summed in bfloat16 or wider, within the bound.
No kernel may reach another device: no remote copies, remote signals or barrier semaphores. Data moves between devices by JAX's collectives and lax.ppermute only.
A program may use at most 128 MiB of HBM per device.

v0:
```python
import math
import jax
import jax.numpy as jnp
from jax import lax
from jax.sharding import PartitionSpec as P

BLOCK = 128


def padded(array, sides, width):
    for axis, dim in sides:
        count, length = (lax.axis_size(axis), array.shape[dim])
        up = [(i, (i + 1) % count) for i in range(count - 1)]
        down = [(j, i) for i, j in up]
        last = lax.slice_in_dim(array, length - width, length, axis=dim)
        initial = lax.slice_in_dim(array, 0, width, axis=dim)
        before = lax.ppermute(last, axis, up)
        after = lax.ppermute(initial, axis, down)
        array = jnp.concatenate([before, array, after], axis=dim)
    return array


def swapped(block, axis, stride):
    count = lax.axis_size(axis)
    route = []
    for low in range(count):
        high = low | 1 << stride
        if high != low and high < count:
            route += [(low, high), (high, low)]
    return lax.ppermute(block, axis, route)


def local(
    probe_vectors,
    mesh_lookup_pair,
    landmark_lookup_pair,
    softmax_warmth,
    output_adjoint,
    exported_boundary_tiles,
    adjacency_tile_filter,
):
    cell_count = probe_vectors.shape[0]
    feat_width = probe_vectors.shape[1]
    block_count = cell_count // BLOCK
    face_count = exported_boundary_tiles.shape[2]
    channel_group_count = softmax_warmth.shape[0]
    channel_width_each = feat_width // channel_group_count
    kv_blocks = mesh_lookup_pair.reshape(block_count, BLOCK, 2, feat_width)
    chosen = exported_boundary_tiles[0]
    picked = kv_blocks[chosen]
    sent_x = jnp.concatenate([picked[0], picked[1]], axis=0)
    rims_x = padded(sent_x, (("gx", 0),), face_count)
    from_lower = rims_x[:face_count]
    from_upper = rims_x[3 * face_count :]
    from_partner = swapped(picked[2], "gy", 0)
    anchors_all = lax.all_gather(landmark_lookup_pair, ("gx", "gy"), axis=0, tiled=True)
    halo_kv = jnp.concatenate([from_lower, from_upper, from_partner], axis=0)
    halo_kv = halo_kv.reshape(3 * face_count * BLOCK, 2, feat_width)
    vicinity_length = cell_count + 3 * face_count * BLOCK
    combined_lookup_pair = jnp.concatenate([mesh_lookup_pair, halo_kv, anchors_all], axis=0)
    anchor_total = anchors_all.shape[0]
    primary_axis_position = lax.axis_index("gx")
    gx_count = lax.axis_size("gx")
    near_mask = (adjacency_tile_filter[0] > 0) | jnp.eye(
        block_count, block_count + 3 * face_count, dtype=bool
    )
    valid = jnp.concatenate(
        [
            jnp.ones((block_count,), bool),
            jnp.full((face_count,), primary_axis_position > 0),
            jnp.full((face_count,), primary_axis_position < gx_count - 1),
            jnp.ones((face_count,), bool),
        ]
    )
    near_mask = near_mask & valid[None]
    near_mask = jnp.repeat(jnp.repeat(near_mask, BLOCK, axis=0), BLOCK, axis=1)
    allowed_couples = jnp.concatenate(
        [near_mask, jnp.ones((cell_count, anchor_total), bool)], axis=1
    )
    logit_multiplier = softmax_warmth / math.sqrt(channel_width_each)
    query_heads = probe_vectors.reshape(cell_count, channel_group_count, channel_width_each)
    grad_heads = output_adjoint.reshape(cell_count, channel_group_count, channel_width_each)
    key_heads = combined_lookup_pair[:, 0].reshape(-1, channel_group_count, channel_width_each)
    value_heads = combined_lookup_pair[:, 1].reshape(-1, channel_group_count, channel_width_each)
    unnormalised_logits = jnp.einsum(
        "qhd,khd->hqk", query_heads, key_heads, preferred_element_type=jnp.float32
    )
    scores = jnp.where(
        allowed_couples[None], unnormalised_logits * logit_multiplier[:, None, None], -jnp.inf
    )
    row_max = jnp.max(scores, axis=2, keepdims=True)
    exp_scores = jnp.exp(scores - row_max)
    weights = exp_scores / jnp.sum(exp_scores, axis=2, keepdims=True)
    weights_b = weights.astype(jnp.bfloat16)
    attended = jnp.einsum(
        "hqk,khd->qhd", weights_b, value_heads, preferred_element_type=jnp.float32
    )
    row_delta = jnp.sum(grad_heads.astype(jnp.float32) * attended, axis=2)
    weight_grad = jnp.einsum(
        "qhd,khd->hqk", grad_heads, value_heads, preferred_element_type=jnp.float32
    )
    logit_adjoint = weights * (weight_grad - jnp.transpose(row_delta)[:, :, None])
    warmth_contribution = jnp.sum(logit_adjoint * unnormalised_logits, axis=(1, 2)) / math.sqrt(
        channel_width_each
    )
    dscore_b = (logit_adjoint * logit_multiplier[:, None, None]).astype(jnp.bfloat16)
    probe_derivative = jnp.einsum(
        "hqk,khd->qhd", dscore_b, key_heads, preferred_element_type=jnp.float32
    )
    probe_derivative = probe_derivative.reshape(cell_count, feat_width).astype(jnp.bfloat16)
    near_key = jnp.einsum(
        "hqk,qhd->khd",
        dscore_b[:, :, :vicinity_length],
        query_heads,
        preferred_element_type=jnp.float32,
    )
    near_value = jnp.einsum(
        "hqk,qhd->khd",
        weights_b[:, :, :vicinity_length],
        grad_heads,
        preferred_element_type=jnp.float32,
    )
    near_terms = jnp.stack(
        [
            near_key.reshape(vicinity_length, feat_width),
            near_value.reshape(vicinity_length, feat_width),
        ],
        axis=1,
    )
    row_total = lax.axis_size(("gx", "gy")) * landmark_lookup_pair.shape[0]
    score_cols = lax.dynamic_slice_in_dim(dscore_b, vicinity_length, row_total, 2)
    weight_cols = lax.dynamic_slice_in_dim(weights_b, vicinity_length, row_total, 2)
    key_part = jnp.einsum(
        "hqk,qhd->khd", score_cols, query_heads, preferred_element_type=jnp.float32
    )
    value_part = jnp.einsum(
        "hqk,qhd->khd", weight_cols, grad_heads, preferred_element_type=jnp.float32
    )
    anchor_grad = lax.psum_scatter(
        jnp.stack(
            [key_part.reshape(row_total, feat_width), value_part.reshape(row_total, feat_width)],
            axis=1,
        ),
        ("gx", "gy"),
        scatter_dimension=0,
        tiled=True,
    )
    face_grads = (
        near_terms[cell_count:].reshape(3, face_count, BLOCK, 2, feat_width).astype(jnp.bfloat16)
    )
    back_sent = jnp.concatenate([face_grads[0], face_grads[1]], axis=0)
    back_x = padded(back_sent, (("gx", 0),), face_count)
    back_partner = swapped(face_grads[2], "gy", 0)
    returned = jnp.stack(
        [back_x[:face_count], back_x[3 * face_count :], back_partner], axis=0
    ).astype(jnp.float32)
    local_blocks = near_terms[:cell_count].reshape(block_count, BLOCK, 2, feat_width)
    block_ids = jnp.arange(block_count, dtype=jnp.int32)
    for direction in range(3):
        hits = (block_ids == chosen[direction, 0]).astype(jnp.float32)
        local_blocks = local_blocks + hits[:, None, None, None] * returned[direction, 0][None]
    cell_grad = local_blocks.reshape(cell_count, 2, feat_width).astype(jnp.bfloat16)
    warmth_derivative = lax.psum(warmth_contribution, ("gx", "gy"))
    return (probe_derivative, cell_grad, anchor_grad, warmth_derivative)


def solution(mesh):
    placed = (
        P(("groups", "gx", "gy"), None),
        P(("groups", "gx", "gy"), None, None),
        P(("groups", "gx", "gy"), None, None),
        P("groups"),
        P(("groups", "gx", "gy"), None),
        P(("groups", "gx", "gy"), None, None),
        P(("groups", "gx", "gy"), None, None),
    )
    return jax.shard_map(
        local,
        mesh=mesh,
        in_specs=placed,
        out_specs=(
            P(("groups", "gx", "gy"), None),
            P(("groups", "gx", "gy"), None, None),
            P(("groups", "gx", "gy"), None, None),
            P("groups"),
        ),
        check_vma=False,
    )
```

profile of v0, /device:TPU:0, one launch (start us, length us, event | category | flops | bytes accessed | tf_op | source)
XLA Modules:
  0.0 289.8 jit_solution(5623075355392274938)
XLA Ops:
  7.2 1.6 copy.115
  8.8 0.7 fusion.27
  9.5 2.2 gather_fusion
  11.7 3.2 %fusion.30 = (bf16[1,128,2,1536]{3,1,2,0:T(8,128)(2,1)}, bf16[1,128,2,1536]{3,1,2,0:T(8,128)(2,1)}, bf16[1,128,2,1536]{3,1,2,0:T(8,128)(2,1)}) fusion(bf16[3,128,2,1536]{3,1,2,0:T(8,128)(2,1)} %gather_fusion), kind=kLoop, calls=%fused_computation.67 | loop fusion | bytes 4718592 | tf_op jit(solution)/shard_map/slice | solution.py:51
  14.9 5.7 %collective-permute-start = (bf16[1,128,2,1536]{3,1,2,0:T(8,128)(2,1)}, bf16[1,128,2,1536]{3,1,2,0:T(8,128)(2,1)}, u32[]{:S(2)}, u32[]{:S(2)}) collective-permute-start(bf16[1,128,2,1536]{3,1,2,0:T(8,128)(2,1)} %get-tuple-element.38), channel_id=1, source_target_pairs={{0,2},{2,4},{4,6},{6,8},{8,10},{10,12},{12,14},{1,3},{3,5},{5,7},{... | collective-permute-start | bytes 2359304 | tf_op jit(solution)/shard_map/ppermute | solution.py:17
  20.6 1.3 collective-permute-start.1
  22.0 0.6 fusion.31
  22.6 46.0 %all_gather.3 = bf16[64,2,1536]{2,1,0:T(2,128)(2,1)S(1)} all-gather(bf16[4,2,1536]{2,1,0:T(2,128)(2,1)S(1)} %copy-done.9), channel_id=1, replica_groups=mesh['groups'=2,'gx'=8,'gy'=2] {'gx','gy'}, dimensions={0}, use_global_device_ids=true | all-gather | bytes 417792 | tf_op jit(solution)/shard_map/all_gather | solution.py:56
  68.8 0.7 compare_convert_fusion
  69.4 0.6 compare_convert_fusion.1
  70.0 1.3 copy.117
  71.3 1.4 copy.120
  72.8 0.7 concatenate.23
  73.5 2.3 copy.124
  75.8 0.6 dynamic-slice
  77.0 0.6 compare_convert_fusion.2
  77.9 2.0 pad_maximum_fusion.2
  80.4 2.3 fusion.29
  82.7 2.8 copy.119
  85.5 4.2 %copy.123 = bf16[704,1,1536]{0,2,1:T(8,128)(2,1)} copy(bf16[704,1,1536]{2,0,1:T(8,128)(2,1)} %get-tuple-element.33) | data formatting | bytes 4325376 | tf_op jit(solution)/shard_map/slice | solution.py:84
  89.7 4.7 %fusion.33 = f32[12,704,256]{2,1,0:T(8,128)} fusion(bf16[704,12,128]{0,2,1:T(8,128)(2,1)S(1)} %bitcast.114, bf16[256,12,128]{0,2,1:T(8,128)(2,1)S(1)} %bitcast.119), kind=kOutput, calls=%fused_computation.70 | convolution fusion | flops 553648128 | bytes 11599872 | tf_op jit(solution)/shard_map/qhd,khd->hqk/dot_general | solution.py:85
  94.4 5.4 %fusion.32 = (f32[12,256]{1,0:T(8,128)S(1)}, f32[12,256,704]{1,2,0:T(8,128)}) fusion(f32[12]{0:T(128)S(1)} %broadcast_multiply_fusion.1, pred[256,704]{0,1:T(8,128)(4,1)S(1)} %copy-done.8, bf16[704,12,128]{0,2,1:T(8,128)(2,1)S(1)} %bitcast.115, bf16[256,12,128]{0,2,1:T(8,128)(2,1)S(1)} %bitcast.120), kind=kOutput, calls=%fused_computation.69 | convolution fusion | flops 562299584 | bytes 11792432 | tf_op jit(solution)/shard_map/sub | solution.py:92
  99.8 4.4 %fusion.15 = bf16[12,256,704]{1,2,0:T(8,128)(2,1)S(1)} fusion(f32[12,256,704]{1,2,0:T(8,128)} %get-tuple-element.45, f32[12,256]{1,0:T(8,128)S(1)} %get-tuple-element.44), kind=kLoop, calls=%fused_computation.23 | loop fusion | flops 4325376 | bytes 12988416 | tf_op jit(solution)/shard_map/convert_element_type | solution.py:94
  104.2 1.1 convolution_bitcast_fusion
  105.4 0.8 fusion.21
  106.2 7.5 %fusion.2 = (f32[12]{0:T(128)S(1)}, bf16[12,256,704]{1,2,0:T(8,128)(2,1)S(1)}) fusion(f32[12,704,256]{2,1,0:T(8,128)} %fusion.33, f32[12]{0:T(128)S(1)} %broadcast_multiply_fusion.1, f32[12,256]{1,0:T(8,128)S(1)} %bitcast.133, bf16[704,12,128]{0,2,1:T(8,128)(2,1)S(1)} %bitcast.131, bf16[256,12,128]{0,2,1:T(8,128)(2,1)S(1)} %bitcast.126, ...), kind=kOutput, calls=%fused_computation.6 | convolution fusion | flops 568786944 | bytes 24600672 | tf_op jit(solution)/shard_map/qhd,khd->hqk/dot_general | solution.py:99
  114.0 3.2 %fusion.13 = f32[12,640,128]{1,2,0:T(8,128)} fusion(bf16[256,12,128]{0,2,1:T(8,128)(2,1)S(1)} %bitcast.122, bf16[12,256,704]{1,2,0:T(8,128)(2,1)S(1)} %get-tuple-element.29), kind=kOutput, calls=%fused_computation.21 | convolution fusion | flops 503316480 | bytes 8650752 | tf_op jit(solution)/shard_map/hqk,qhd->khd/dot_general | solution.py:111
  117.2 3.2 %fusion.11 = f32[12,640,128]{1,2,0:T(8,128)} fusion(bf16[256,12,128]{0,2,1:T(8,128)(2,1)S(1)} %bitcast.127, bf16[12,256,704]{1,2,0:T(8,128)(2,1)S(1)} %fusion.15), kind=kOutput, calls=%fused_computation.19 | convolution fusion | flops 503316480 | bytes 8650752 | tf_op jit(solution)/shard_map/hqk,qhd->khd/dot_general | solution.py:117
  120.7 1.2 copy.136
  121.9 0.8 stack_reshape.15
  122.7 9.1 %copy.131 = f32[640,1,1536]{2,1,0:T(1,128)} copy(f32[640,1,1536]{0,2,1:T(8,128)} %bitcast.117) | data formatting | bytes 7864320 | tf_op jit(solution)/shard_map/stack;reshape | solution.py:123
  131.8 9.2 %copy.132 = f32[640,1,1536]{2,1,0:T(1,128)} copy(f32[640,1,1536]{0,2,1:T(8,128)} %bitcast.118) | data formatting | bytes 7864320 | tf_op jit(solution)/shard_map/stack;reshape | solution.py:123
  141.0 12.3 %fusion.3 = bf16[640,2,1536]{2,1,0:T(2,128)(2,1)} fusion(f32[640,1,1536]{2,1,0:T(1,128)} %copy.132, f32[640,1,1536]{2,1,0:T(1,128)} %copy.131), kind=kLoop, calls=%fused_computation.12 | loop fusion | flops 7864320 | bytes 11796480 | tf_op jit(solution)/shard_map/convert
  153.3 3.8 %slice_bitcast_fusion.5 = (bf16[1,128,2,1536]{3,2,1,0:T(2,128)(2,1)}, bf16[1,128,2,1536]{3,2,1,0:T(2,128)(2,1)}, bf16[1,128,2,1536]{3,2,1,0:T(2,128)(2,1)}) fusion(bf16[640,2,1536]{2,1,0:T(2,128)(2,1)} %fusion.3), kind=kLoop, calls=%fused_computation.44 | loop fusion | bytes 4718592 | tf_op jit(solution)/shard_map/squeeze | solution.py:151
  157.1 4.2 %collective-permute-start.3 = (bf16[1,128,2,1536]{3,2,1,0:T(2,128)(2,1)}, bf16[1,128,2,1536]{3,2,1,0:T(2,128)(2,1)}, u32[]{:S(2)}, u32[]{:S(2)}) collective-permute-start(bf16[1,128,2,1536]{3,2,1,0:T(2,128)(2,1)} %get-tuple-element.35), channel_id=1, source_target_pairs={{0,2},{2,4},{4,6},{6,8},{8,10},{10,12},{12,14},{1,3},{3,5},{5,7},{... | collective-permute-start | bytes 2359304 | tf_op jit(solution)/shard_map/ppermute | solution.py:17
  161.3 1.3 collective-permute-start.4
  162.7 1.0 pad_maximum_fusion.3
  163.7 55.9 %psum.7 = f32[12]{0:T(128)} all-reduce(f32[12]{0:T(128)S(1)} %broadcast_multiply_fusion), channel_id=1, replica_groups=mesh['groups'=2,'gx'=8,'gy'=2] {'gx','gy'}, use_global_device_ids=true, to_apply=%region_5.6 | all-reduce | flops 12 | bytes 96 | tf_op jit(solution)/shard_map/psum | solution.py:163
  219.5 3.0 %convolution_convert_fusion = bf16[12,128,256]{2,1,0:T(8,128)(2,1)S(1)} fusion(bf16[704,12,128]{0,2,1:T(8,128)(2,1)S(1)} %bitcast.116, bf16[12,256,704]{1,2,0:T(8,128)(2,1)} %copy-done.2), kind=kOutput, calls=%fused_computation.39 | convolution fusion | flops 554041344 | bytes 7274496 | tf_op jit(solution)/shard_map/hqk,khd->qhd/dot_general | solution.py:107
  222.5 1.2 copy.137
  223.7 42.1 %all-reduce.4.cloned.1.call-done = f32[64,2,1536]{2,0,1:T(8,128)} async-done(((f32[64,2,1536]{2,0,1:T(8,128)}), f32[64,2,1536]{2,0,1:T(8,128)}) %all-reduce.4.cloned.1.call-update) | async-done | bytes 786448
  265.8 0.9 constant_dynamic-slice_fusion
  266.7 0.6 copy.138
  267.4 5.1 %maximum_convert_fusion = f32[3,1,128,2,1536]{4,3,2,1,0:T(2,128)S(1)} fusion(bf16[1,1,128,2,1536]{4,3,2,1,0:T(2,128)(2,1)} %bitcast.30, bf16[1,1,128,2,1536]{4,3,2,1,0:T(2,128)(2,1)} %bitcast.28, bf16[1,1,128,2,1536]{4,3,2,1,0:T(2,128)(2,1)} %bitcast.26), kind=kLoop, calls=%fused_computation.33 | loop fusion | flops 3538944 | bytes 7077888 | tf_op jit(solution)/shard_map/convert_element_type | solution.py:156
  272.5 1.7 slice_bitcast_fusion.2
  274.2 0.4 copy-done
  274.6 1.2 copy-done.1
  275.8 7.2 %fusion.20 = bf16[256,2,1536]{2,1,0:T(2,128)(2,1)} fusion(f32[640,1,1536]{2,1,0:T(1,128)S(1)} %copy-done.1, f32[640,1,1536]{2,1,0:T(1,128)S(1)} %copy-done, f32[256]{0:T(256)S(1)} %get-tuple-element.46, f32[256]{0:T(256)S(1)} %get-tuple-element.47, f32[256]{0:T(256)S(1)} %broadcast_bitcast_fusion.3, f32[128,2,1536]{2,1,0:T(2,128)S(1)} %get-tuple-element.31, ...), kind=kLoop, calls=%fused_computation.29 | loop fusion | flops 6291456 | bytes 14158848 | tf_op jit(solution)/shard_map/convert_element_type | solution.py:162
  (52 shorter events, 2.0 us)
Async XLA Ops:
  7.2 258.6 %all-reduce.4.cloned.1.call-start = ((), (), s32[]{:S(2)}) async-start(), calls=%async_computation | async-start | bytes 1572864
  9.5 12.5 %copy-start.10 = (s32[1,3,1]{1,2,0:T(1,128)S(1)}, s32[1,3,1]{1,2,0:T(1,128)}, u32[]{:S(2)}) copy-start(s32[1,3,1]{1,2,0:T(1,128)} %param.12) | copy-start | bytes 40
  9.5 13.1 %copy-start.9 = (bf16[4,2,1536]{2,1,0:T(2,128)(2,1)S(1)}, bf16[4,2,1536]{2,1,0:T(2,128)(2,1)}, u32[]{:S(2)}) copy-start(bf16[4,2,1536]{2,1,0:T(2,128)(2,1)} %param.9) | copy-start | bytes 73732
  9.5 59.2 %copy-start.11 = (s32[1,2,5]{2,1,0:T(2,128)S(1)}, s32[1,2,5]{2,1,0:T(2,128)}, u32[]{:S(2)}) copy-start(s32[1,2,5]{2,1,0:T(2,128)} %param.13) | copy-start | bytes 124
  11.7 58.3 %copy-start.4 = (bf16[256,2,1536]{2,1,0:T(2,128)(2,1)S(1)}, bf16[256,2,1536]{2,1,0:T(2,128)(2,1)}, u32[]{:S(2)}) copy-start(bf16[256,2,1536]{2,1,0:T(2,128)(2,1)} %param.8) | copy-start | bytes 4718596
  14.9 63.0 %collective-permute-start = (bf16[1,128,2,1536]{3,1,2,0:T(8,128)(2,1)}, bf16[1,128,2,1536]{3,1,2,0:T(8,128)(2,1)}, u32[]{:S(2)}, u32[]{:S(2)}) collective-permute-start(bf16[1,128,2,1536]{3,1,2,0:T(8,128)(2,1)} %get-tuple-element.38), channel_id=1, source_target_pairs={{0,2},{2,4},{4,6},{6,8},{8,10},{10,12},{12,14},{1,3},{3,5},{5,7},{... | collective-permute-start | bytes 2359304 | tf_op jit(solution)/shard_map/ppermute | solution.py:17
  20.6 57.2 %collective-permute-start.1 = (bf16[1,128,2,1536]{3,1,2,0:T(8,128)(2,1)}, bf16[1,128,2,1536]{3,1,2,0:T(8,128)(2,1)}, u32[]{:S(2)}, u32[]{:S(2)}) collective-permute-start(bf16[1,128,2,1536]{3,1,2,0:T(8,128)(2,1)} %get-tuple-element.39), channel_id=1, source_target_pairs={{2,0},{4,2},{6,4},{8,6},{10,8},{12,10},{14,12},{3,1},{5,3},{7,5},{... | collective-permute-start | bytes 2359304 | tf_op jit(solution)/shard_map/ppermute | solution.py:18
  21.9 56.0 %collective-permute-start.2 = (bf16[1,128,2,1536]{3,1,2,0:T(8,128)(2,1)}, bf16[1,128,2,1536]{3,1,2,0:T(8,128)(2,1)}, u32[]{:S(2)}, u32[]{:S(2)}) collective-permute-start(bf16[1,128,2,1536]{3,1,2,0:T(8,128)(2,1)} %get-tuple-element.40), channel_id=1, source_target_pairs={{0,1},{1,0},{2,3},{3,2},{4,5},{5,4},{6,7},{7,6},{8,9},{9,8},{10,11... | collective-permute-start | bytes 2359304 | tf_op jit(solution)/shard_map/ppermute | solution.py:30
  22.6 53.2 %copy-start.13 = (u32[32]{0:T(128)S(1)}, u32[32]{0:T(128)}, u32[]{:S(2)}) copy-start(u32[32]{0:T(128)} %constant.34) | copy-start | bytes 388
  68.6 9.1 %copy-start.12 = (f32[12]{0:T(128)S(1)}, f32[12]{0:T(128)}, u32[]{:S(2)}) copy-start(f32[12]{0:T(128)} %param.10) | copy-start | bytes 148
  77.8 2.3 copy-start.5
  89.7 4.7 %copy-start.8 = (pred[256,704]{0,1:T(8,128)(4,1)S(1)}, pred[256,704]{0,1:T(8,128)(4,1)}, u32[]{:S(2)}) copy-start(pred[256,704]{0,1:T(8,128)(4,1)} %concatenate.23) | copy-start | bytes 540676
  99.8 4.4 %copy-start.3 = (bf16[256,1536]{0,1:T(8,128)(2,1)S(1)}, bf16[256,1536]{0,1:T(8,128)(2,1)}, u32[]{:S(2)}) copy-start(bf16[256,1536]{0,1:T(8,128)(2,1)} %copy.124) | copy-start | bytes 2359300
  99.8 5.6 %copy-start.6 = (bf16[704,1,1536]{0,2,1:T(8,128)(2,1)S(1)}, bf16[704,1,1536]{0,2,1:T(8,128)(2,1)}, u32[]{:S(2)}) copy-start(bf16[704,1,1536]{0,2,1:T(8,128)(2,1)} %copy.123) | copy-start | bytes 6488068
  113.6 3.6 %copy-start.2 = (bf16[12,256,704]{1,2,0:T(8,128)(2,1)}, bf16[12,256,704]{1,2,0:T(8,128)(2,1)S(1)}, u32[]{:S(2)}) copy-start(bf16[12,256,704]{1,2,0:T(8,128)(2,1)S(1)} %get-tuple-element.29) | copy-start | bytes 12976132
  153.3 9.4 %copy-start.7 = (f32[64,1,1536]{2,0,1:T(8,128)S(1)}, f32[64,1,1536]{2,0,1:T(8,128)}, u32[]{:S(2)}) copy-start(f32[64,1,1536]{2,0,1:T(8,128)} %stack_reshape.15) | copy-start | bytes 1179652
  157.1 110.2 %collective-permute-start.3 = (bf16[1,128,2,1536]{3,2,1,0:T(2,128)(2,1)}, bf16[1,128,2,1536]{3,2,1,0:T(2,128)(2,1)}, u32[]{:S(2)}, u32[]{:S(2)}) collective-permute-start(bf16[1,128,2,1536]{3,2,1,0:T(2,128)(2,1)} %get-tuple-element.35), channel_id=1, source_target_pairs={{0,2},{2,4},{4,6},{6,8},{8,10},{10,12},{12,14},{1,3},{3,5},{5,7},{... | collective-permute-start | bytes 2359304 | tf_op jit(solution)/shard_map/ppermute | solution.py:17
  161.3 106.1 %collective-permute-start.4 = (bf16[1,128,2,1536]{3,2,1,0:T(2,128)(2,1)}, bf16[1,128,2,1536]{3,2,1,0:T(2,128)(2,1)}, u32[]{:S(2)}, u32[]{:S(2)}) collective-permute-start(bf16[1,128,2,1536]{3,2,1,0:T(2,128)(2,1)} %get-tuple-element.37), channel_id=1, source_target_pairs={{2,0},{4,2},{6,4},{8,6},{10,8},{12,10},{14,12},{3,1},{5,3},{7,5},{... | collective-permute-start | bytes 2359304 | tf_op jit(solution)/shard_map/ppermute | solution.py:18
  162.6 104.8 %collective-permute-start.5 = (bf16[1,128,2,1536]{3,2,1,0:T(2,128)(2,1)}, bf16[1,128,2,1536]{3,2,1,0:T(2,128)(2,1)}, u32[]{:S(2)}, u32[]{:S(2)}) collective-permute-start(bf16[1,128,2,1536]{3,2,1,0:T(2,128)(2,1)} %get-tuple-element.36), channel_id=1, source_target_pairs={{0,1},{1,0},{2,3},{3,2},{4,5},{5,4},{6,7},{7,6},{8,9},{9,8},{10,11... | collective-permute-start | bytes 2359304 | tf_op jit(solution)/shard_map/ppermute | solution.py:30
  272.5 2.1 copy-start
  272.5 3.3 %copy-start.1 = (f32[640,1,1536]{2,1,0:T(1,128)S(1)}, f32[640,1,1536]{2,1,0:T(1,128)}, u32[]{:S(2)}) copy-start(f32[640,1,1536]{2,1,0:T(1,128)} %copy.132) | copy-start | bytes 11796484
Sparse Core Ops, SparseCore 0:
  163.8 101.9 all-reduce.3
where the time goes:
time: 291 us; the launch traced here: 290 us
  blocking collectives  102 us (35%)
  local copies, waits for them, and re-layouts  54.1 us (19%)
  waiting for transfers between devices  42.1 us (14%)
  other arithmetic  34.9 us (12%)
  matrix products  29.2 us (10%)
  between operations  15 us (5%)
  starting transfers between devices  12.7 us (4%)
    psum x1, blocking collectives, local(): warmth_derivative = lax.psum(warmth_contribution, ('gx', 'gy'))  55.9 us
    all_gather x1, blocking collectives, local(): lax.all_gather(landmark_lookup_pair, ('gx', 'gy'), axis=0, tiled=True)  46 us
    unnamed x2, waiting for transfers between devices  42.1 us
    another operation x2, local copies, waits for them, and re-layouts, local(): jnp.stack([near_key.reshape(vicinity_length, feat_width), near_value.resh...  18.3 us
    another operation x1, other arithmetic  12.3 us
    unnamed x35, local copies, waits for them, and re-layouts  9.96 us
    ppermute x2, starting transfers between devices, padded(): before = lax.ppermute(last, axis, up)  9.89 us
    dot_general x1, matrix products, local(): jnp.einsum('qhd,khd->hqk', grad_heads, value_heads, preferred_element_typ...  7.46 us
  transfers between devices with their start and end apart: 7, of which 1 were waited for; matrix products, arithmetic and copies ran while one was open for 5% of the time, Pallas kernels for 0%

commit v1 on v0

--- a/solution.py
+++ b/solution.py
@@ -160,7 +160,7 @@
         hits = (block_ids == chosen[direction, 0]).astype(jnp.float32)
         local_blocks = local_blocks + hits[:, None, None, None] * returned[direction, 0][None]
     cell_grad = local_blocks.reshape(cell_count, 2, feat_width).astype(jnp.bfloat16)
-    warmth_derivative = lax.psum(warmth_contribution, ("gx", "gy"))
+    warmth_derivative = jnp.sum(lax.all_gather(warmth_contribution, ("gx", "gy")), axis=0)
     return (probe_derivative, cell_grad, anchor_grad, warmth_derivative)
 
 

time: 291 us -> 245 us (0.84)
  waiting for transfers between devices: 42.1 us -> 1.34 us
  blocking collectives: 102 us -> 96.9 us
    psum x1 -> x0, blocking collectives: 55.9 us -> none  [local(): warmth_derivative = lax.psum(warmth_contribution, ('gx', 'gy'))]
    unnamed x0 -> x1, blocking collectives: none -> 51 us
    unnamed x2, waiting for transfers between devices: 42.1 us -> 1.32 us
    unnamed x35 -> x42, local copies, waits for them, and re-layouts: 9.96 us -> 8.81 us
  transfers between devices with their start and end apart: 7 -> 7, of which waited for: 1 -> 1; matrix products, arithmetic and copies ran while one was open for 5% -> 20% of each run, Pallas kernels for 0% -> 0%
where the time goes in v1:
time: 245 us; the launch traced here: 244 us
  blocking collectives  96.9 us (40%)
  local copies, waits for them, and re-layouts  52.3 us (21%)
  other arithmetic  36.4 us (15%)
  matrix products  28.9 us (12%)
  between operations  15.7 us (6%)
  starting transfers between devices  12.6 us (5%)
    unnamed x1, blocking collectives  51 us
    all_gather x1, blocking collectives, local(): lax.all_gather(landmark_lookup_pair, ('gx', 'gy'), axis=0, tiled=True)  45.9 us
    another operation x2, local copies, waits for them, and re-layouts, local(): jnp.stack([near_key.reshape(vicinity_length, feat_width), near_value.resh...  18.2 us
    another operation x1, other arithmetic  12.3 us
    ppermute x2, starting transfers between devices, padded(): before = lax.ppermute(last, axis, up)  9.83 us
    unnamed x42, local copies, waits for them, and re-layouts  8.81 us
    dot_general x1, matrix products, local(): jnp.einsum('qhd,khd->hqk', grad_heads, value_heads, preferred_element_typ...  7.97 us
    convert_element_type x1, other arithmetic, local(): local_blocks.reshape(cell_count, 2, feat_width).astype(jnp.bfloat16)  7.09 us
  transfers between devices with their start and end apart: 7, of which 1 were waited for; matrix products, arithmetic and copies ran while one was open for 20% of the time, Pallas kernels for 0%

profile of v1, /device:TPU:0, one launch (start us, length us, event | category | flops | bytes accessed | tf_op | source)
XLA Modules:
  0.0 244.2 jit_solution(4354792471489366205)
XLA Ops:
  7.2 1.6 copy.140
  8.8 0.7 fusion.27
  9.5 2.2 gather_fusion
  11.7 3.1 %fusion.30 = (bf16[1,128,2,1536]{3,1,2,0:T(8,128)(2,1)}, bf16[1,128,2,1536]{3,1,2,0:T(8,128)(2,1)}, bf16[1,128,2,1536]{3,1,2,0:T(8,128)(2,1)}) fusion(bf16[3,128,2,1536]{3,1,2,0:T(8,128)(2,1)} %gather_fusion), kind=kLoop, calls=%fused_computation.67 | loop fusion | bytes 4718592 | tf_op jit(solution)/shard_map/slice | solution.py:51
  14.8 5.7 %collective-permute-start = (bf16[1,128,2,1536]{3,1,2,0:T(8,128)(2,1)}, bf16[1,128,2,1536]{3,1,2,0:T(8,128)(2,1)}, u32[]{:S(2)}, u32[]{:S(2)}) collective-permute-start(bf16[1,128,2,1536]{3,1,2,0:T(8,128)(2,1)} %get-tuple-element.42), channel_id=1, source_target_pairs={{0,2},{2,4},{4,6},{6,8},{8,10},{10,12},{12,14},{1,3},{3,5},{5,7},{... | collective-permute-start | bytes 2359304 | tf_op jit(solution)/shard_map/ppermute | solution.py:17
  20.5 1.3 collective-permute-start.1
  21.9 0.7 fusion.32
  22.5 45.9 %all_gather.7 = bf16[64,2,1536]{2,1,0:T(2,128)(2,1)S(1)} all-gather(bf16[4,2,1536]{2,1,0:T(2,128)(2,1)S(1)} %copy-done.6), channel_id=1, replica_groups=mesh['groups'=2,'gx'=8,'gy'=2] {'gx','gy'}, dimensions={0}, use_global_device_ids=true | all-gather | bytes 417792 | tf_op jit(solution)/shard_map/all_gather | solution.py:56
  68.7 0.6 compare_convert_fusion
  69.2 0.7 compare_convert_fusion.1
  70.2 1.4 copy.145
  71.6 2.3 copy.149
  73.9 0.6 fusion.31
  75.8 0.6 compare_convert_fusion.2
  76.5 0.7 broadcast_bitcast_fusion.3
  77.2 0.6 broadcast_bitcast_fusion.1
  77.8 1.9 pad_maximum_fusion.2
  80.2 2.3 fusion.29
  82.4 2.8 %copy.144 = bf16[704,1,1536]{0,2,1:T(8,128)(2,1)S(1)} copy(bf16[704,1,1536]{2,0,1:T(8,128)(2,1)} %get-tuple-element.38) | data formatting | bytes 4325376 | tf_op jit(solution)/shard_map/slice | solution.py:83
  85.2 4.2 %copy.148 = bf16[704,1,1536]{0,2,1:T(8,128)(2,1)} copy(bf16[704,1,1536]{2,0,1:T(8,128)(2,1)} %get-tuple-element.37) | data formatting | bytes 4325376 | tf_op jit(solution)/shard_map/slice | solution.py:84
  89.4 4.7 %fusion.34 = f32[12,704,256]{2,1,0:T(8,128)} fusion(bf16[704,12,128]{0,2,1:T(8,128)(2,1)S(1)} %bitcast.115, bf16[256,12,128]{0,2,1:T(8,128)(2,1)S(1)} %bitcast.120), kind=kOutput, calls=%fused_computation.71 | convolution fusion | flops 553648128 | bytes 11599872 | tf_op jit(solution)/shard_map/qhd,khd->hqk/dot_general | solution.py:85
  94.1 5.4 %fusion.33 = (f32[12,256]{1,0:T(8,128)S(1)}, f32[12,256,704]{1,2,0:T(8,128)}) fusion(f32[12]{0:T(128)S(1)} %broadcast_multiply_fusion, pred[256,704]{0,1:T(8,128)(4,1)S(1)} %concatenate.23, bf16[704,12,128]{0,2,1:T(8,128)(2,1)S(1)} %bitcast.116, bf16[256,12,128]{0,2,1:T(8,128)(2,1)S(1)} %bitcast.121), kind=kOutput, calls=%fused_computation.70 | convolution fusion | flops 562299584 | bytes 11792432 | tf_op jit(solution)/shard_map/sub | solution.py:92
  99.5 4.4 %fusion.15 = bf16[12,256,704]{1,2,0:T(8,128)(2,1)S(1)} fusion(f32[12,256,704]{1,2,0:T(8,128)} %get-tuple-element.51, f32[12,256]{1,0:T(8,128)S(1)} %get-tuple-element.50), kind=kLoop, calls=%fused_computation.23 | loop fusion | flops 4325376 | bytes 12988416 | tf_op jit(solution)/shard_map/convert_element_type | solution.py:94
  104.4 0.8 fusion.21
  105.2 8.0 %fusion.2 = (f32[12]{0:T(128)}, bf16[12,256,704]{1,2,0:T(8,128)(2,1)S(1)}) fusion(f32[12,704,256]{2,1,0:T(8,128)} %fusion.34, f32[12]{0:T(128)S(1)} %copy-done.16, f32[12,256]{1,0:T(8,128)S(1)} %bitcast.134, bf16[704,12,128]{0,2,1:T(8,128)(2,1)S(1)} %bitcast.132, bf16[256,12,128]{0,2,1:T(8,128)(2,1)S(1)} %bitcast.127, ...), kind=kOutput, calls=%fused_computation.6 | convolution fusion | flops 568786944 | bytes 24600672 | tf_op jit(solution)/shard_map/qhd,khd->hqk/dot_general | solution.py:99
  113.2 0.4 convolution_bitcast_fusion.1
  113.5 3.2 %fusion.13 = f32[12,640,128]{1,2,0:T(8,128)} fusion(bf16[256,12,128]{0,2,1:T(8,128)(2,1)S(1)} %bitcast.123, bf16[12,256,704]{1,2,0:T(8,128)(2,1)S(1)} %get-tuple-element.33), kind=kOutput, calls=%fused_computation.21 | convolution fusion | flops 503316480 | bytes 8650752 | tf_op jit(solution)/shard_map/hqk,qhd->khd/dot_general | solution.py:111
  116.7 3.1 %fusion.11 = f32[12,640,128]{1,2,0:T(8,128)} fusion(bf16[256,12,128]{0,2,1:T(8,128)(2,1)S(1)} %bitcast.128, bf16[12,256,704]{1,2,0:T(8,128)(2,1)S(1)} %fusion.15), kind=kOutput, calls=%fused_computation.19 | convolution fusion | flops 503316480 | bytes 8650752 | tf_op jit(solution)/shard_map/hqk,qhd->khd/dot_general | solution.py:117
  120.1 0.8 stack_reshape.14
  121.2 1.9 pad_maximum_fusion.3
  123.2 9.1 %copy.156 = f32[640,1,1536]{2,1,0:T(1,128)} copy(f32[640,1,1536]{0,2,1:T(8,128)} %bitcast.118) | data formatting | bytes 7864320 | tf_op jit(solution)/shard_map/stack;reshape | solution.py:123
  132.3 9.1 %copy.157 = f32[640,1,1536]{2,1,0:T(1,128)} copy(f32[640,1,1536]{0,2,1:T(8,128)} %bitcast.119) | data formatting | bytes 7864320 | tf_op jit(solution)/shard_map/stack;reshape | solution.py:123
  141.4 12.3 %fusion.3 = bf16[640,2,1536]{2,1,0:T(2,128)(2,1)} fusion(f32[640,1,1536]{2,1,0:T(1,128)} %copy.157, f32[640,1,1536]{2,1,0:T(1,128)} %copy.156), kind=kLoop, calls=%fused_computation.12 | loop fusion | flops 7864320 | bytes 11796480 | tf_op jit(solution)/shard_map/convert
  153.7 3.8 %slice_bitcast_fusion.5 = (bf16[1,128,2,1536]{3,2,1,0:T(2,128)(2,1)}, bf16[1,128,2,1536]{3,2,1,0:T(2,128)(2,1)}, bf16[1,128,2,1536]{3,2,1,0:T(2,128)(2,1)}) fusion(bf16[640,2,1536]{2,1,0:T(2,128)(2,1)} %fusion.3), kind=kLoop, calls=%fused_computation.44 | loop fusion | bytes 4718592 | tf_op jit(solution)/shard_map/squeeze | solution.py:151
  157.5 4.1 %collective-permute-start.3 = (bf16[1,128,2,1536]{3,2,1,0:T(2,128)(2,1)}, bf16[1,128,2,1536]{3,2,1,0:T(2,128)(2,1)}, u32[]{:S(2)}, u32[]{:S(2)}) collective-permute-start(bf16[1,128,2,1536]{3,2,1,0:T(2,128)(2,1)} %get-tuple-element.39), channel_id=1, source_target_pairs={{0,2},{2,4},{4,6},{6,8},{8,10},{10,12},{12,14},{1,3},{3,5},{5,7},{... | collective-permute-start | bytes 2359304 | tf_op jit(solution)/shard_map/ppermute | solution.py:17
  161.6 1.3 collective-permute-start.4
  163.1 3.0 %convolution_convert_fusion = bf16[12,128,256]{2,1,0:T(8,128)(2,1)S(1)} fusion(bf16[704,12,128]{0,2,1:T(8,128)(2,1)S(1)} %bitcast.117, bf16[12,256,704]{1,2,0:T(8,128)(2,1)} %copy-done.2), kind=kOutput, calls=%fused_computation.39 | convolution fusion | flops 554041344 | bytes 7274496 | tf_op jit(solution)/shard_map/hqk,khd->qhd/dot_general | solution.py:107
  166.1 1.2 copy.162
  167.3 51.0 %all-reduce.1 = f32[192]{0:T(256)S(1)} all-reduce(f32[192]{0:T(256)S(1)} %multiply_dynamic-update-slice_fusion), channel_id=2, replica_groups=mesh['groups'=2,'gx'=8,'gy'=2] {'gx','gy'}, use_global_device_ids=true, to_apply=%add.1 | all-reduce | flops 192 | bytes 1536
  218.4 0.5 reduce_sum.39
  218.9 1.3 all-reduce.5.cloned.1.call-done
  220.2 0.9 constant_dynamic-slice_fusion
  221.1 0.6 copy.163
  221.8 5.1 %maximum_convert_fusion = f32[3,1,128,2,1536]{4,3,2,1,0:T(2,128)S(1)} fusion(bf16[1,1,128,2,1536]{4,3,2,1,0:T(2,128)(2,1)} %bitcast.30, bf16[1,1,128,2,1536]{4,3,2,1,0:T(2,128)(2,1)} %bitcast.28, bf16[1,1,128,2,1536]{4,3,2,1,0:T(2,128)(2,1)} %bitcast.26), kind=kLoop, calls=%fused_computation.33 | loop fusion | flops 3538944 | bytes 7077888 | tf_op jit(solution)/shard_map/convert_element_type | solution.py:156
  227.0 1.7 slice_bitcast_fusion.2
  228.7 0.4 copy-done
  229.0 1.2 copy-done.1
  230.3 7.1 %fusion.20 = bf16[256,2,1536]{2,1,0:T(2,128)(2,1)} fusion(f32[640,1,1536]{2,1,0:T(1,128)S(1)} %copy-done.1, f32[640,1,1536]{2,1,0:T(1,128)S(1)} %copy-done, f32[256]{0:T(256)S(1)} %copy-done.8, f32[256]{0:T(256)S(1)} %copy-done.9, f32[256]{0:T(256)S(1)} %copy-done.11, f32[128,2,1536]{2,1,0:T(2,128)S(1)} %get-tuple-element.35, ...), kind=kLoop, calls=%fused_computation.29 | loop fusion | flops 6291456 | bytes 14158848 | tf_op jit(solution)/shard_map/convert_element_type | solution.py:162
  (61 shorter events, 2.4 us)
Async XLA Ops:
  7.2 213.1 %all-reduce.5.cloned.1.call-start = ((), (), s32[]{:S(2)}) async-start(), calls=%async_computation | async-start | bytes 1572864
  9.5 12.4 %copy-start.7 = (s32[1,3,1]{1,2,0:T(1,128)S(1)}, s32[1,3,1]{1,2,0:T(1,128)}, u32[]{:S(2)}) copy-start(s32[1,3,1]{1,2,0:T(1,128)} %param.12) | copy-start | bytes 40
  9.5 59.1 %copy-start.12 = (s32[1,2,5]{2,1,0:T(2,128)S(1)}, s32[1,2,5]{2,1,0:T(2,128)}, u32[]{:S(2)}) copy-start(s32[1,2,5]{2,1,0:T(2,128)} %param.13) | copy-start | bytes 124
  9.5 60.4 %copy-start.4 = (bf16[256,2,1536]{2,1,0:T(2,128)(2,1)S(1)}, bf16[256,2,1536]{2,1,0:T(2,128)(2,1)}, u32[]{:S(2)}) copy-start(bf16[256,2,1536]{2,1,0:T(2,128)(2,1)} %param.8) | copy-start | bytes 4718596
  11.7 10.8 %copy-start.6 = (bf16[4,2,1536]{2,1,0:T(2,128)(2,1)S(1)}, bf16[4,2,1536]{2,1,0:T(2,128)(2,1)}, u32[]{:S(2)}) copy-start(bf16[4,2,1536]{2,1,0:T(2,128)(2,1)} %param.9) | copy-start | bytes 73732
  14.8 63.0 %collective-permute-start = (bf16[1,128,2,1536]{3,1,2,0:T(8,128)(2,1)}, bf16[1,128,2,1536]{3,1,2,0:T(8,128)(2,1)}, u32[]{:S(2)}, u32[]{:S(2)}) collective-permute-start(bf16[1,128,2,1536]{3,1,2,0:T(8,128)(2,1)} %get-tuple-element.42), channel_id=1, source_target_pairs={{0,2},{2,4},{4,6},{6,8},{8,10},{10,12},{12,14},{1,3},{3,5},{5,7},{... | collective-permute-start | bytes 2359304 | tf_op jit(solution)/shard_map/ppermute | solution.py:17
  20.5 57.3 %collective-permute-start.1 = (bf16[1,128,2,1536]{3,1,2,0:T(8,128)(2,1)}, bf16[1,128,2,1536]{3,1,2,0:T(8,128)(2,1)}, u32[]{:S(2)}, u32[]{:S(2)}) collective-permute-start(bf16[1,128,2,1536]{3,1,2,0:T(8,128)(2,1)} %get-tuple-element.43), channel_id=1, source_target_pairs={{2,0},{4,2},{6,4},{8,6},{10,8},{12,10},{14,12},{3,1},{5,3},{7,5},{... | collective-permute-start | bytes 2359304 | tf_op jit(solution)/shard_map/ppermute | solution.py:18
  21.8 56.0 %collective-permute-start.2 = (bf16[1,128,2,1536]{3,1,2,0:T(8,128)(2,1)}, bf16[1,128,2,1536]{3,1,2,0:T(8,128)(2,1)}, u32[]{:S(2)}, u32[]{:S(2)}) collective-permute-start(bf16[1,128,2,1536]{3,1,2,0:T(8,128)(2,1)} %get-tuple-element.44), channel_id=1, source_target_pairs={{0,1},{1,0},{2,3},{3,2},{4,5},{5,4},{6,7},{7,6},{8,9},{9,8},{10,11... | collective-permute-start | bytes 2359304 | tf_op jit(solution)/shard_map/ppermute | solution.py:30
  22.5 51.4 %copy-start.10 = (u32[32]{0:T(128)S(1)}, u32[32]{0:T(128)}, u32[]{:S(2)}) copy-start(u32[32]{0:T(128)} %constant.34) | copy-start | bytes 388
  68.5 8.0 %copy-start.13 = (f32[12]{0:T(128)S(1)}, f32[12]{0:T(128)}, u32[]{:S(2)}) copy-start(f32[12]{0:T(128)} %param.10) | copy-start | bytes 148
  76.5 17.6 %copy-start.15 = (f32[12]{0:T(128)}, f32[12]{0:T(128)S(1)}, u32[]{:S(2)}) copy-start(f32[12]{0:T(128)S(1)} %broadcast_multiply_fusion) | copy-start | bytes 148
  99.5 4.4 %copy-start.3 = (bf16[256,1536]{0,1:T(8,128)(2,1)S(1)}, bf16[256,1536]{0,1:T(8,128)(2,1)}, u32[]{:S(2)}) copy-start(bf16[256,1536]{0,1:T(8,128)(2,1)} %copy.149) | copy-start | bytes 2359300
  99.5 4.8 %copy-start.5 = (bf16[704,1,1536]{0,2,1:T(8,128)(2,1)S(1)}, bf16[704,1,1536]{0,2,1:T(8,128)(2,1)}, u32[]{:S(2)}) copy-start(bf16[704,1,1536]{0,2,1:T(8,128)(2,1)} %copy.148) | copy-start | bytes 6488068
  104.3 0.8 copy-start.16
  113.1 3.6 %copy-start.2 = (bf16[12,256,704]{1,2,0:T(8,128)(2,1)}, bf16[12,256,704]{1,2,0:T(8,128)(2,1)S(1)}, u32[]{:S(2)}) copy-start(bf16[12,256,704]{1,2,0:T(8,128)(2,1)S(1)} %get-tuple-element.33) | copy-start | bytes 12976132
  157.5 64.3 %collective-permute-start.3 = (bf16[1,128,2,1536]{3,2,1,0:T(2,128)(2,1)}, bf16[1,128,2,1536]{3,2,1,0:T(2,128)(2,1)}, u32[]{:S(2)}, u32[]{:S(2)}) collective-permute-start(bf16[1,128,2,1536]{3,2,1,0:T(2,128)(2,1)} %get-tuple-element.39), channel_id=1, source_target_pairs={{0,2},{2,4},{4,6},{6,8},{8,10},{10,12},{12,14},{1,3},{3,5},{5,7},{... | collective-permute-start | bytes 2359304 | tf_op jit(solution)/shard_map/ppermute | solution.py:17
  161.6 60.2 %collective-permute-start.4 = (bf16[1,128,2,1536]{3,2,1,0:T(2,128)(2,1)}, bf16[1,128,2,1536]{3,2,1,0:T(2,128)(2,1)}, u32[]{:S(2)}, u32[]{:S(2)}) collective-permute-start(bf16[1,128,2,1536]{3,2,1,0:T(2,128)(2,1)} %get-tuple-element.41), channel_id=1, source_target_pairs={{2,0},{4,2},{6,4},{8,6},{10,8},{12,10},{14,12},{3,1},{5,3},{7,5},{... | collective-permute-start | bytes 2359304 | tf_op jit(solution)/shard_map/ppermute | solution.py:18
  162.9 4.3 %copy-start.14 = (f32[12]{0:T(128)S(1)}, f32[12]{0:T(128)}, u32[]{:S(2)}) copy-start(f32[12]{0:T(128)} %get-tuple-element.32) | copy-start | bytes 148
  162.9 58.9 %collective-permute-start.5 = (bf16[1,128,2,1536]{3,2,1,0:T(2,128)(2,1)}, bf16[1,128,2,1536]{3,2,1,0:T(2,128)(2,1)}, u32[]{:S(2)}, u32[]{:S(2)}) collective-permute-start(bf16[1,128,2,1536]{3,2,1,0:T(2,128)(2,1)} %get-tuple-element.40), channel_id=1, source_target_pairs={{0,1},{1,0},{2,3},{3,2},{4,5},{5,4},{6,7},{7,6},{8,9},{9,8},{10,11... | collective-permute-start | bytes 2359304 | tf_op jit(solution)/shard_map/ppermute | solution.py:30
  226.9 2.1 copy-start
  226.9 3.3 %copy-start.1 = (f32[640,1,1536]{2,1,0:T(1,128)S(1)}, f32[640,1,1536]{2,1,0:T(1,128)}, u32[]{:S(2)}) copy-start(f32[640,1,1536]{2,1,0:T(1,128)} %copy.157) | copy-start | bytes 11796484
  227.0 3.3 %copy-start.8 = (f32[256]{0:T(256)S(1)}, f32[256]{0:T(256)}, u32[]{:S(2)}) copy-start(f32[256]{0:T(256)} %get-tuple-element.52) | copy-start | bytes 3076
  227.0 3.3 %copy-start.9 = (f32[256]{0:T(256)S(1)}, f32[256]{0:T(256)}, u32[]{:S(2)}) copy-start(f32[256]{0:T(256)} %get-tuple-element.53) | copy-start | bytes 3076
  227.0 3.3 %copy-start.11 = (f32[256]{0:T(256)S(1)}, f32[256]{0:T(256)}, u32[]{:S(2)}) copy-start(f32[256]{0:T(256)} %broadcast_bitcast_fusion.3) | copy-start | bytes 3076
Sparse Core Ops, SparseCore 0:
  123.3 96.8 all-reduce.4
